TPU v7x, 256 devices: a whole 4x4x8 slice. The times are simulated.
256 devices in a mesh: blk: 32 (over y, z_hi, core), ij: 8 (over z_lo, x).
Axes of the slice: x: 4, y: 4, z: 8 (z_hi: 4, z_lo: 2; z = z_hi * 2 + z_lo), core: 2. Of those that a mesh axis runs over, the one named last changes fastest.
Arguments:
- density: float32 [32, 6, 256, 128], P('blk', None, 'ij'), may hold values from 0.8 to 1.2
- momentum: float32 [32, 3, 6, 256, 128], P('blk', None, None, 'ij'), may hold values from -2.5 to 2.5
- energy: float32 [32, 6, 256, 128], P('blk', None, 'ij'), may hold values from 2.5 to 4
- metrics: float32 [32, 4, 256, 128], P('blk', None, 'ij'), may hold values from -1 to 1
- volume: float32 [32, 256, 128], P('blk', 'ij'), may hold values from 0.5 to 2
- placed: int32 [32], replicated, may hold values from 0 to 31, each once
- neighbour: int32 [32, 2], replicated, may hold values from 0 to 31, as said below
- face: int32 [32, 2], replicated, may hold values from 0 to 1, as said below
- orient: int32 [32, 2], replicated, may hold values from 0 to 1, as said below
Outputs:
- next_density: float32 [32, 6, 256, 128], P('blk', None, 'ij')
- next_momentum: float32 [32, 3, 6, 256, 128], P('blk', None, None, 'ij')
- next_energy: float32 [32, 6, 256, 128], P('blk', None, 'ij')
Inputs may be any that keep to these rules, and one draw needn't show every extreme that they name: If face f of block b meets face g of block c with orientation o, then face g of c meets face f of b with orientation o; every block id appears as a neighbour. `face`: consistent with neighbour as stated there. `orient`: consistent with neighbour as stated there.
All inputs are finite; a program needn't handle non-finite values.
Results may differ from a plain program's by a relative error of at most 0.00002.
Values sent between devices are 32-bit elements; how exact they have to be, the bound alone decides.
A program may use at most 128 MiB of HBM per device.

v0:
```python
import jax
import jax.numpy as jnp
from jax import lax
from jax.sharding import PartitionSpec as P

pressure_factor = 0.4
viscosity = 0.05
conduction = 0.1
time_step = 0.03


def extended(value, sides, width):
    for axis, dim in sides:
        size, length = (lax.axis_size(axis), value.shape[dim])
        up = [(i, (i + 1) % size) for i in range(size - 1)]
        down = [(j, i) for i, j in up]
        last = lax.slice_in_dim(value, length - width, length, axis=dim)
        initial = lax.slice_in_dim(value, 0, width, axis=dim)
        before = lax.ppermute(last, axis, up)
        after = lax.ppermute(initial, axis, down)
        value = jnp.concatenate([before, value, after], axis=dim)
    return value


def slope_rows(f):
    return (
        f[..., 0:-4, 2:-2] - 8.0 * f[..., 1:-3, 2:-2] + 8.0 * f[..., 3:-1, 2:-2] - f[..., 4:, 2:-2]
    ) / 12.0


def slope_cols(f):
    return (
        f[..., 2:-2, 0:-4] - 8.0 * f[..., 2:-2, 1:-3] + 8.0 * f[..., 2:-2, 3:-1] - f[..., 2:-2, 4:]
    ) / 12.0


def slope_planes(f):
    return (
        jnp.roll(f, 2, -3)
        - 8.0 * jnp.roll(f, 1, -3)
        + 8.0 * jnp.roll(f, -1, -3)
        - jnp.roll(f, -2, -3)
    ) / 12.0


def curve_rows(f):
    return (
        -f[..., 0:-4, 2:-2]
        + 16.0 * f[..., 1:-3, 2:-2]
        - 30.0 * f[..., 2:-2, 2:-2]
        + 16.0 * f[..., 3:-1, 2:-2]
        - f[..., 4:, 2:-2]
    ) / 12.0


def curve_cols(f):
    return (
        -f[..., 2:-2, 0:-4]
        + 16.0 * f[..., 2:-2, 1:-3]
        - 30.0 * f[..., 2:-2, 2:-2]
        + 16.0 * f[..., 2:-2, 3:-1]
        - f[..., 2:-2, 4:]
    ) / 12.0


def curve_planes(f):
    return (
        -jnp.roll(f, 2, -3)
        + 16.0 * jnp.roll(f, 1, -3)
        - 30.0 * f
        + 16.0 * jnp.roll(f, -1, -3)
        - jnp.roll(f, -2, -3)
    ) / 12.0


def interior(f):
    return f[..., 2:-2, 2:-2]


def residual(ext):
    planes = ext.shape[1] - 1
    fields = ext[:, :planes]
    metric = ext[:, planes]
    dens = fields[0]
    moment = fields[1:4]
    energy_now = fields[4]
    velocity = moment / dens
    kinetic = 0.5 * jnp.sum(moment * velocity, axis=0)
    pressure = pressure_factor * (energy_now - kinetic)
    thermal = pressure / dens
    total_head = energy_now + pressure
    row_ax, row_ay, col_bx, col_by, cell_vol = (
        metric[0],
        metric[1],
        metric[2],
        metric[3],
        metric[4],
    )
    along_rows = row_ax * velocity[0] + row_ay * velocity[1]
    along_cols = col_bx * velocity[0] + col_by * velocity[1]
    flux_rows = cell_vol * jnp.stack(
        [
            dens * along_rows,
            moment[0] * along_rows + row_ax * pressure,
            moment[1] * along_rows + row_ay * pressure,
            moment[2] * along_rows,
            total_head * along_rows,
        ]
    )
    flux_cols = cell_vol * jnp.stack(
        [
            dens * along_cols,
            moment[0] * along_cols + col_bx * pressure,
            moment[1] * along_cols + col_by * pressure,
            moment[2] * along_cols,
            total_head * along_cols,
        ]
    )
    flux_planes = jnp.stack(
        [
            moment[2],
            moment[0] * velocity[2],
            moment[1] * velocity[2],
            moment[2] * velocity[2] + pressure,
            total_head * velocity[2],
        ]
    )
    inviscid = -(slope_rows(flux_rows) + slope_cols(flux_cols)) / interior(cell_vol) - slope_planes(
        interior(flux_planes)
    )
    row_weight = interior(row_ax * row_ax + row_ay * row_ay)
    col_weight = interior(col_bx * col_bx + col_by * col_by)

    def laplace(w):
        return row_weight * curve_rows(w) + col_weight * curve_cols(w) + curve_planes(interior(w))

    half_speed = kinetic / dens
    diffuse = jnp.stack(
        [
            jnp.zeros_like(inviscid[0]),
            viscosity * laplace(velocity[0]),
            viscosity * laplace(velocity[1]),
            viscosity * laplace(velocity[2]),
            viscosity * laplace(half_speed) + conduction * laplace(thermal),
        ]
    )
    return inviscid + diffuse


def wall_signs(planes):
    channel = jnp.arange(5)[:, None]
    plane_index = jnp.arange(planes)[None, :]
    flipped = (channel >= 1) & (channel <= 3) & (plane_index < planes - 1)
    return jnp.where(flipped, -1.0, 1.0)[:, :, None, None]


def ghost_factors(twisted, facing, planes):
    own_face = jnp.arange(2)[None, :]
    turn = jnp.where(twisted == 1, -1.0, 1.0)
    same = jnp.where(facing == own_face, -1.0, 1.0)
    channel = jnp.arange(5)[None, None, :]
    by_channel = jnp.where(
        channel < 2, turn[:, :, None], jnp.where(channel < 4, same[:, :, None], 1.0)
    )
    metric_plane = (jnp.arange(planes) == planes - 1)[None, None, None, :]
    return jnp.where(metric_plane, by_channel[:, :, :, None], 1.0)


def locate(placed):
    blocks = placed.shape[0]
    slots = jnp.arange(blocks, dtype=jnp.int32)
    return jnp.sum(jnp.where(placed[:, None] == slots[None, :], slots[:, None], 0), axis=0)


def pick_faces(target, facing, piece):
    piece_rows = piece.shape[0]
    slot_index = jnp.arange(piece_rows, dtype=jnp.int32)
    matched = target[:, :, None] == slot_index[None, None, :]
    chosen = jnp.where(
        facing[:, :, None, None, None, None, None] == 1,
        piece[None, None, :, 1],
        piece[None, None, :, 0],
    )
    return jnp.sum(jnp.where(matched[:, :, :, None, None, None, None], chosen, 0.0), axis=2)


def local(density, momentum, energy, metrics, volume, placed, neighbour, face, orient):
    local_count = density.shape[0]
    planes = density.shape[1] + 1
    fields = jnp.concatenate([density[:, None], momentum, energy[:, None]], axis=1)
    metric_plane = jnp.concatenate([metrics, volume[:, None]], axis=1)[:, :, None]
    split_count = lax.axis_size("ij")
    split_index = lax.axis_index("ij")
    group_index = lax.axis_index("blk")
    position = group_index * local_count + jnp.arange(local_count, dtype=jnp.int32)
    own_ids = placed[position]
    position_of = locate(placed)
    next_ids = neighbour[own_ids]
    facing = face[own_ids]
    twisted = orient[own_ids]
    partner = position_of[next_ids]
    factor = ghost_factors(twisted, facing, planes)[:, :, None, :, :, None]
    signs = wall_signs(planes)

    def extend(base):
        padded = extended(base, (("ij", 3),), 2)
        low_wall = base[:, :, :, 1::-1] * signs
        high_wall = base[:, :, :, -1:-3:-1]
        low_rows = jnp.where(split_index == 0, low_wall, padded[:, :, :, 0:2])
        high_rows = jnp.where(split_index == split_count - 1, high_wall, padded[:, :, :, -2:])
        rowed = jnp.concatenate([low_rows, base, high_rows], axis=3)
        strips = jnp.moveaxis(jnp.stack([base[..., 0:2], base[..., -1:-3:-1]], axis=1), -1, 2)
        source = partner // local_count * split_count + jnp.where(
            twisted == 1, split_count - 1 - split_index, split_index
        )
        target = source * local_count + partner % local_count
        ghosts = pick_faces(
            target, facing, lax.all_gather(strips, ("blk", "ij"), axis=0, tiled=True)
        )
        ghosts = jnp.where(twisted[:, :, None, None, None, None] == 1, ghosts[..., ::-1], ghosts)
        ghosts = jnp.moveaxis(ghosts * factor, 2, -1)
        left = jnp.pad(
            ghosts[:, 0][..., ::-1], ((0, 0), (0, 0), (0, 0), (2, 2), (0, 0)), constant_values=1.0
        )
        right = jnp.pad(ghosts[:, 1], ((0, 0), (0, 0), (0, 0), (2, 2), (0, 0)), constant_values=1.0)
        return jnp.concatenate([left, rowed, right], axis=-1)

    def tendency(state):
        return jax.vmap(residual)(extend(jnp.concatenate([state, metric_plane], axis=2)))

    section = fields + time_step * tendency(fields)
    result = 0.5 * fields + 0.5 * (section + time_step * tendency(section))
    return (result[:, 0], result[:, 1:4], result[:, 4])


def solution(mesh):
    return jax.shard_map(
        local,
        mesh=mesh,
        in_specs=(
            P("blk", None, "ij", None),
            P("blk", None, None, "ij", None),
            P("blk", None, "ij", None),
            P("blk", None, "ij", None),
            P("blk", "ij", None),
            P(),
            P(),
            P(),
            P(),
        ),
        out_specs=(
            P("blk", None, "ij", None),
            P("blk", None, None, "ij", None),
            P("blk", None, "ij", None),
        ),
        check_vma=False,
    )
```

profile of v0, /device:TPU:99, one launch (start us, length us, event | category | flops | bytes accessed | tf_op | source)
XLA Modules:
  0.0 1607.6 jit_solution(9384204103739592441)
XLA Ops:
  7.2 0.9 fusion.228
  8.1 1.1 fusion.49
  10.6 0.7 maximum_bitcast_fusion
  11.5 3.1 collective-permute-start
  14.6 2.2 collective-permute-start.1
  22.1 733.1 %all-gather.3.cloned.1.call-done = f32[256,2,2,5,7,32]{5,2,4,3,1,0:T(2,128)} async-done(((f32[1,2,2,5,7,32]{5,2,4,3,1,0:T(2,128)}), f32[256,2,2,5,7,32]{5,2,4,3,1,0:T(2,128)}) %all-gather.3.cloned.1.call-update) | async-done | bytes 4587536 | tf_op jit(solution)/shard_map/all_gather | solution.py:218
  755.1 18.2 %slice_bitcast_fusion.3 = (f32[256,2,5,7,32]{4,1,3,2,0:T(2,128)}, f32[256,2,5,7,32]{4,1,3,2,0:T(2,128)}) fusion(f32[256,2,2,5,7,32]{5,2,4,3,1,0:T(2,128)} %all-gather.3.cloned.1.call-done), kind=kLoop, calls=%fused_computation.4 | loop fusion | bytes 9175040 | tf_op jit(solution)/shard_map/jit(_where)/broadcast_in_dim | solution.py:179
  773.4 9.6 copy.248
  782.9 11.1 copy.249
  794.1 2.6 select_reduce_fusion.1
  797.4 0.8 select_maximum_fusion.2
  798.2 0.8 fusion.281
  803.3 0.9 fusion.170
  804.2 0.9 fusion.157
  805.1 0.9 fusion.144
  806.0 1.1 fusion.120
  807.2 2.1 multiply_add_fusion
  810.7 0.7 maximum_bitcast_fusion.1
  812.2 1.9 collective-permute-start.3
  814.1 3.5 collective-permute-start.2
  817.9 0.9 collective-permute-done.2
  818.9 729.0 %all-gather.5.cloned.1.call-done = f32[256,2,2,5,7,32]{5,2,4,3,1,0:T(2,128)} async-done(((f32[1,2,2,5,7,32]{5,2,4,3,1,0:T(2,128)}), f32[256,2,2,5,7,32]{5,2,4,3,1,0:T(2,128)}) %all-gather.5.cloned.1.call-update) | async-done | bytes 4587536 | tf_op jit(solution)/shard_map/all_gather | solution.py:218
  1548.0 18.2 %slice_bitcast_fusion.1 = (f32[256,2,5,7,32]{4,1,3,2,0:T(2,128)}, f32[256,2,5,7,32]{4,1,3,2,0:T(2,128)}) fusion(f32[256,2,2,5,7,32]{5,2,4,3,1,0:T(2,128)} %all-gather.5.cloned.1.call-done), kind=kLoop, calls=%fused_computation.2 | loop fusion | bytes 9175040 | tf_op jit(solution)/shard_map/jit(_where)/broadcast_in_dim | solution.py:179
  1566.2 9.6 copy.281
  1575.8 11.1 copy.282
  1586.9 2.6 select_reduce_fusion
  1590.3 0.8 select_maximum_fusion
  1591.1 0.8 fusion.280
  1596.1 0.9 copy-done.5
  1598.3 1.0 add_multiply_fusion
  1599.3 0.7 slice.1499
  1600.0 0.7 slice_bitcast_fusion.26
  (175 shorter events, 18.2 us)
Async XLA Ops:
  7.2 12.2 copy-start
  7.2 747.9 %all-gather.3.cloned.1.call-start = ((), (), s32[]{:S(2)}) async-start(), calls=%async_computation | async-start | bytes 18421760 | tf_op jit(solution)/shard_map/all_gather | solution.py:218
  10.4 6.5 copy-start.8
  10.4 9.2 copy-start.6
  10.6 9.8 copy-start.7
  11.4 1536.6 %all-gather.5.cloned.1.call-start = ((), (), s32[]{:S(2)}) async-start(), calls=%async_computation.1 | async-start | bytes 18421760 | tf_op jit(solution)/shard_map/all_gather | solution.py:218
  11.5 10.5 collective-permute-start
  14.6 7.3 collective-permute-start.1
  806.0 1.1 copy-start.2
  806.0 1.1 copy-start.3
  806.0 1.1 copy-start.4
  812.2 5.7 collective-permute-start.3
  814.1 4.7 collective-permute-start.2
  1595.9 1.0 copy-start.5
  1598.3 2.4 copy-start.1
Sparse Core Ops, SparseCore 0:
  11.5 743.6 all-gather.2
  811.5 736.3 all-gather.4
where the time goes:
time: 1610 us
  waiting for transfers between devices  1460 us (91%)
  local copies, waits for them, and re-layouts  92.8 us (6%)
  other arithmetic  24 us (1%)
  between operations  16.8 us (1%)
    all_gather x2, waiting for transfers between devices, extend(): lax.all_gather(strips, ('blk', 'ij'), axis=0, tiled=True)  1460 us
    broadcast_in_dim x6, local copies, waits for them, and re-layouts, pick_faces(): jnp.where(facing[:, :, None, None, None, None, None] == 1, piece[None, No...  77.9 us
  transfers between devices with their start and end apart: 6, of which 3 were waited for; matrix products, arithmetic and copies ran while one was open for 0% of the time, Pallas kernels for 0%

commit v1 on v0

--- a/solution.py
+++ b/solution.py
@@ -7,6 +7,11 @@
 viscosity = 0.05
 conduction = 0.1
 time_step = 0.03
+
+
+def swapped_in(x, axis, along):
+    sent = jnp.stack([x] * lax.axis_size(axis))
+    return jnp.concatenate(lax.all_to_all(sent, axis, 0, 0), axis=along)
 
 
 def extended(value, sides, width):
@@ -214,9 +219,7 @@
             twisted == 1, split_count - 1 - split_index, split_index
         )
         target = source * local_count + partner % local_count
-        ghosts = pick_faces(
-            target, facing, lax.all_gather(strips, ("blk", "ij"), axis=0, tiled=True)
-        )
+        ghosts = pick_faces(target, facing, swapped_in(strips, ("blk", "ij"), 0))
         ghosts = jnp.where(twisted[:, :, None, None, None, None] == 1, ghosts[..., ::-1], ghosts)
         ghosts = jnp.moveaxis(ghosts * factor, 2, -1)
         left = jnp.pad(

time: 1610 us -> 489 us (0.30)
  the two profiles are of different devices: /device:TPU:99 before, /device:TPU:1 now
where the time goes in v1:
time: 489 us; the launch traced here: 479 us
  waiting for transfers between devices  200 us (41%)
  local copies, waits for them, and re-layouts  190 us (39%)
  other arithmetic  51.5 us (11%)
  starting transfers between devices  34.1 us (7%)
    all_to_all x2, waiting for transfers between devices, swapped_in(): return jnp.concatenate(lax.all_to_all(sent, axis, 0, 0), axis=along)  193 us
    unnamed x27, local copies, waits for them, and re-layouts  95.4 us
    broadcast_in_dim x6, local copies, waits for them, and re-layouts, pick_faces(): jnp.where(facing[:, :, None, None, None, None, None] == 1, piece[None, No...  65.4 us
    all_to_all x2, other arithmetic, swapped_in(): return jnp.concatenate(lax.all_to_all(sent, axis, 0, 0), axis=along)  31.3 us
    all_to_all x2, starting transfers between devices, swapped_in(): return jnp.concatenate(lax.all_to_all(sent, axis, 0, 0), axis=along)  24.3 us
    reshape x2, local copies, waits for them, and re-layouts, swapped_in(): return jnp.concatenate(lax.all_to_all(sent, axis, 0, 0), axis=along)  16.9 us
  transfers between devices with their start and end apart: 6, of which 4 were waited for; matrix products, arithmetic and copies ran while one was open for 1% of the time, Pallas kernels for 0%

profile of v1, /device:TPU:1, one launch (start us, length us, event | category | flops | bytes accessed | tf_op | source)
XLA Modules:
  0.0 478.9 jit_solution(17619554864893886509)
XLA Ops:
  0.6 0.9 fusion.228
  1.5 1.1 fusion.49
  4.1 6.7 %broadcast_bitcast_fusion.1 = f32[256,1,2,5,7,2,32]{6,5,4,3,2,1,0:T(2,128)} fusion(f32[2,2,5,7,32]{4,1,3,2,0:T(2,128)S(1)} %maximum_bitcast_fusion), kind=kLoop, calls=%fused_computation.607 | loop fusion | bytes 4605440
  10.8 21.2 %reshape.2210 = f32[256,1,4480]{2,1,0:T(1,128)} reshape(f32[256,1,2,5,7,2,32]{6,5,4,3,2,1,0:T(2,128)} %broadcast_bitcast_fusion.1) | data formatting | bytes 9175040
  32.0 16.5 %all-to-all-start = ((f32[256,1,4480]{2,1,0:T(1,128)}), f32[256,1,4480]{2,1,0:T(1,128)}, u32[]{:S(2)}, u32[]{:S(2)}) async-start(f32[256,1,4480]{2,1,0:T(1,128)} %reshape.2210), calls=%async_computation | async-start | bytes 9175040 | tf_op jit(solution)/shard_map/all_to_all | solution.py:14
  48.7 3.3 collective-permute-start
  52.0 1.3 collective-permute-start.1
  57.6 1.6 collective-permute-done.1
  59.4 96.5 %all-to-all-done = f32[256,1,4480]{2,1,0:T(1,128)} async-done(((f32[256,1,4480]{2,1,0:T(1,128)}), f32[256,1,4480]{2,1,0:T(1,128)}, u32[]{:S(2)}, u32[]{:S(2)}) %all-to-all-start) | async-done | bytes 4587552 | tf_op jit(solution)/shard_map/all_to_all | solution.py:14
  156.4 15.6 %reduce.10 = f32[256,4480]{1,0:T(8,128)} reduce(f32[256,1,4480]{2,1,0:T(1,128)} %all-to-all-done, f32[]{:T(128)} %broadcast.1245), dimensions={1}, to_apply=%all_to_all.6.reduce_sub_computation | reduce | bytes 9175044 | tf_op jit(solution)/shard_map/all_to_all | solution.py:14
  172.0 19.0 %reshape.2211 = f32[256,1,2,5,7,2,32]{6,5,4,3,2,1,0:T(2,128)} reshape(f32[256,4480]{1,0:T(8,128)} %reduce.10) | data formatting | bytes 9175040
  191.0 8.4 %bitcast_bitcast_fusion.1 = f32[256,2,2,5,7,32]{5,2,4,3,1,0:T(2,128)S(1)} fusion(f32[256,1,2,5,7,2,32]{6,5,4,3,2,1,0:T(2,128)} %reshape.2211), kind=kLoop, calls=%fused_computation.605 | loop fusion | bytes 9175040 | tf_op jit(solution)/shard_map/reshape | solution.py:14
  199.4 10.2 %slice_bitcast_fusion.3 = (f32[256,2,5,7,32]{4,1,3,2,0:T(2,128)}, f32[256,2,5,7,32]{4,1,3,2,0:T(2,128)}) fusion(f32[256,2,2,5,7,32]{5,2,4,3,1,0:T(2,128)S(1)} %bitcast_bitcast_fusion.1), kind=kLoop, calls=%fused_computation.4 | loop fusion | bytes 9175040 | tf_op jit(solution)/shard_map/jit(_where)/broadcast_in_dim | solution.py:184
  209.6 11.1 %copy.244 = f32[256,2,5,7,32]{0,4,3,2,1:T(8,128)} copy(f32[256,2,5,7,32]{4,1,3,2,0:T(2,128)} %get-tuple-element.68) | data formatting | bytes 4587520 | tf_op jit(solution)/shard_map/jit(_where)/broadcast_in_dim | solution.py:184
  220.7 11.5 %copy.245 = f32[256,2,5,7,32]{0,4,3,2,1:T(8,128)} copy(f32[256,2,5,7,32]{4,1,3,2,0:T(2,128)} %get-tuple-element.69) | data formatting | bytes 4587520 | tf_op jit(solution)/shard_map/jit(_where)/broadcast_in_dim | solution.py:184
  232.3 3.1 select_reduce_fusion.1
  243.9 1.0 multiply_add_fusion
  246.4 6.7 %broadcast_bitcast_fusion = f32[256,1,2,5,7,2,32]{6,5,4,3,2,1,0:T(2,128)} fusion(f32[2,2,5,7,32]{4,1,3,2,0:T(2,128)S(1)} %maximum_bitcast_fusion.1), kind=kLoop, calls=%fused_computation.606 | loop fusion | bytes 4605440
  253.1 21.2 %reshape.2212 = f32[256,1,4480]{2,1,0:T(1,128)} reshape(f32[256,1,2,5,7,2,32]{6,5,4,3,2,1,0:T(2,128)} %broadcast_bitcast_fusion) | data formatting | bytes 9175040
  274.3 7.7 %all-to-all-start.1 = ((f32[256,1,4480]{2,1,0:T(1,128)}), f32[256,1,4480]{2,1,0:T(1,128)}, u32[]{:S(2)}, u32[]{:S(2)}) async-start(f32[256,1,4480]{2,1,0:T(1,128)} %reshape.2212), calls=%async_computation.1 | async-start | bytes 9175040 | tf_op jit(solution)/shard_map/all_to_all | solution.py:14
  282.1 1.3 collective-permute-start.3
  283.5 4.0 collective-permute-start.2
  287.6 5.1 %collective-permute-done.3 = f32[1,5,7,2,128]{4,3,2,1,0:T(2,128)S(1)} collective-permute-done((f32[1,5,7,2,128]{4,3,2,1,0:T(2,128)S(1)}, f32[1,5,7,2,128]{4,3,2,1,0:T(2,128)S(1)}, u32[]{:S(2)}, u32[]{:S(2)}) %collective-permute-start.3) | collective-permute-done | bytes 35872 | tf_op jit(solution)/shard_map/ppermute | solution.py:25
  292.9 96.6 %all-to-all-done.1 = f32[256,1,4480]{2,1,0:T(1,128)} async-done(((f32[256,1,4480]{2,1,0:T(1,128)}), f32[256,1,4480]{2,1,0:T(1,128)}, u32[]{:S(2)}, u32[]{:S(2)}) %all-to-all-start.1) | async-done | bytes 4587552 | tf_op jit(solution)/shard_map/all_to_all | solution.py:14
  389.5 15.6 %reduce.11 = f32[256,4480]{1,0:T(8,128)} reduce(f32[256,1,4480]{2,1,0:T(1,128)} %all-to-all-done.1, f32[]{:T(128)} %broadcast.1245), dimensions={1}, to_apply=%all_to_all.7.reduce_sub_computation | reduce | bytes 9175044 | tf_op jit(solution)/shard_map/all_to_all | solution.py:14
  405.2 19.0 %reshape.2213 = f32[256,1,2,5,7,2,32]{6,5,4,3,2,1,0:T(2,128)} reshape(f32[256,4480]{1,0:T(8,128)} %reduce.11) | data formatting | bytes 9175040
  424.1 8.4 %bitcast_bitcast_fusion = f32[256,2,2,5,7,32]{5,2,4,3,1,0:T(2,128)S(1)} fusion(f32[256,1,2,5,7,2,32]{6,5,4,3,2,1,0:T(2,128)} %reshape.2213), kind=kLoop, calls=%fused_computation.604 | loop fusion | bytes 9175040 | tf_op jit(solution)/shard_map/reshape | solution.py:14
  432.6 10.2 %slice_bitcast_fusion.1 = (f32[256,2,5,7,32]{4,1,3,2,0:T(2,128)}, f32[256,2,5,7,32]{4,1,3,2,0:T(2,128)}) fusion(f32[256,2,2,5,7,32]{5,2,4,3,1,0:T(2,128)S(1)} %bitcast_bitcast_fusion), kind=kLoop, calls=%fused_computation.2 | loop fusion | bytes 9175040 | tf_op jit(solution)/shard_map/jit(_where)/broadcast_in_dim | solution.py:184
  442.7 11.1 %copy.277 = f32[256,2,5,7,32]{0,4,3,2,1:T(8,128)} copy(f32[256,2,5,7,32]{4,1,3,2,0:T(2,128)} %get-tuple-element.66) | data formatting | bytes 4587520 | tf_op jit(solution)/shard_map/jit(_where)/broadcast_in_dim | solution.py:184
  453.9 11.3 %copy.278 = f32[256,2,5,7,32]{0,4,3,2,1:T(8,128)} copy(f32[256,2,5,7,32]{4,1,3,2,0:T(2,128)} %get-tuple-element.67) | data formatting | bytes 4587520 | tf_op jit(solution)/shard_map/jit(_where)/broadcast_in_dim | solution.py:184
  465.2 3.1 select_reduce_fusion
  476.2 1.0 add_multiply_fusion
  (180 shorter events, 23.7 us)
Async XLA Ops:
  32.0 123.9 %all-to-all-start = ((f32[256,1,4480]{2,1,0:T(1,128)}), f32[256,1,4480]{2,1,0:T(1,128)}, u32[]{:S(2)}, u32[]{:S(2)}) async-start(f32[256,1,4480]{2,1,0:T(1,128)} %reshape.2210), calls=%async_computation | async-start | bytes 9175040 | tf_op jit(solution)/shard_map/all_to_all | solution.py:14
  48.5 4.8 copy-start.6
  48.5 7.3 %copy-start.3 = (s32[32,2]{0,1:T(2,128)S(1)}, s32[32,2]{0,1:T(2,128)}, u32[]{:S(2)}) copy-start(s32[32,2]{0,1:T(2,128)} %param.16) | copy-start | bytes 772
  48.6 7.3 %copy-start.4 = (s32[32,2]{0,1:T(2,128)S(1)}, s32[32,2]{0,1:T(2,128)}, u32[]{:S(2)}) copy-start(s32[32,2]{0,1:T(2,128)} %param.15) | copy-start | bytes 772
  48.6 8.3 %copy-start.5 = (s32[32,2]{0,1:T(2,128)S(1)}, s32[32,2]{0,1:T(2,128)}, u32[]{:S(2)}) copy-start(s32[32,2]{0,1:T(2,128)} %param.17) | copy-start | bytes 772
  48.7 10.6 %collective-permute-start = (f32[1,5,7,2,128]{4,3,2,1,0:T(2,128)S(1)}, f32[1,5,7,2,128]{4,3,2,1,0:T(2,128)S(1)}, u32[]{:S(2)}, u32[]{:S(2)}) collective-permute-start(f32[1,5,7,2,128]{4,3,2,1,0:T(2,128)S(1)} %slice.1247), channel_id=1, source_target_pairs={{0,1},{1,2},{2,3},{3,4},{4,5},{5,6},{6,7},{8,9},{9,10},{10,11},{11... | collective-permute-start | bytes 107528 | tf_op jit(solution)/shard_map/ppermute | solution.py:24
  52.0 7.3 %collective-permute-start.1 = (f32[1,5,7,2,128]{4,3,2,1,0:T(2,128)S(1)}, f32[1,5,7,2,128]{4,3,2,1,0:T(2,128)S(1)}, u32[]{:S(2)}, u32[]{:S(2)}) collective-permute-start(f32[1,5,7,2,128]{4,3,2,1,0:T(2,128)S(1)} %fusion.282), channel_id=1, source_target_pairs={{1,0},{2,1},{3,2},{4,3},{5,4},{6,5},{7,6},{9,8},{10,9},{11,10},{12... | collective-permute-start | bytes 107528 | tf_op jit(solution)/shard_map/ppermute | solution.py:25
  242.8 1.0 copy-start
  242.9 1.0 copy-start.1
  242.9 1.0 copy-start.2
  274.3 115.2 %all-to-all-start.1 = ((f32[256,1,4480]{2,1,0:T(1,128)}), f32[256,1,4480]{2,1,0:T(1,128)}, u32[]{:S(2)}, u32[]{:S(2)}) async-start(f32[256,1,4480]{2,1,0:T(1,128)} %reshape.2212), calls=%async_computation.1 | async-start | bytes 9175040 | tf_op jit(solution)/shard_map/all_to_all | solution.py:14
  282.1 10.6 %collective-permute-start.3 = (f32[1,5,7,2,128]{4,3,2,1,0:T(2,128)S(1)}, f32[1,5,7,2,128]{4,3,2,1,0:T(2,128)S(1)}, u32[]{:S(2)}, u32[]{:S(2)}) collective-permute-start(f32[1,5,7,2,128]{4,3,2,1,0:T(2,128)S(1)} %get-tuple-element.110), channel_id=1, source_target_pairs={{1,0},{2,1},{3,2},{4,3},{5,4},{6,5},{7,6},{9,8},{10,9},{11,10},{12... | collective-permute-start | bytes 107528 | tf_op jit(solution)/shard_map/ppermute | solution.py:25
  283.5 9.3 %collective-permute-start.2 = (f32[1,5,7,2,128]{4,3,2,1,0:T(2,128)S(1)}, f32[1,5,7,2,128]{4,3,2,1,0:T(2,128)S(1)}, u32[]{:S(2)}, u32[]{:S(2)}) collective-permute-start(f32[1,5,7,2,128]{4,3,2,1,0:T(2,128)S(1)} %fusion.230), channel_id=1, source_target_pairs={{0,1},{1,2},{2,3},{3,4},{4,5},{5,6},{6,7},{8,9},{9,10},{10,11},{11... | collective-permute-start | bytes 107528 | tf_op jit(solution)/shard_map/ppermute | solution.py:24
